TPU v7x, 256 devices: a whole 4x4x8 slice. The times are simulated.
256 devices in a mesh: grid: 16 (over y, x), day: 16 (over z, core).
Axes of the slice: x: 4, y: 4, z: 8, core: 2. Of those that a mesh axis runs over, the one named last changes fastest.
Arguments:
- anomalies: bfloat16 [16384, 65536], P('day', 'grid'), may hold values from -6 to 6
- eofs: bfloat16 [64, 65536], P(None, ('grid', 'day')), may hold values from -0.0234375 to 0.0234375
- means_init: float32 [8, 64], replicated, may hold values from -4 to 4
- variances: float32 [8, 64], replicated, may hold values from 0.05 to 2
- mixing: float32 [8], replicated, may hold values from 0.5 to 2
Outputs:
- regime_means: float32 [8, 64], replicated
- regime_covs: float32 [8, 64, 64], replicated
- regime_weights: float32 [8], replicated
- membership: float32 [8, 16384], P(None, 'day')
- composites: bfloat16 [8, 65536], P(None, ('grid', 'day'))
All inputs are finite; a program needn't handle non-finite values.
Results may differ from a plain program's by a relative error of at most 0.0034.
Values may be sent and summed in bfloat16 or wider, within the bound.
No kernel may reach another device: no remote copies, remote signals or barrier semaphores. Data moves between devices by JAX's collectives and lax.ppermute only.
A program may use at most 64 MiB of HBM per device.

v0:
```python
import jax
import jax.numpy as jnp
from jax import lax
from jax.sharding import PartitionSpec as P

ITERS = 2
PRECISE = lax.Precision.HIGHEST
REG = 0.01


def log_density(pcs_t, means, covs, weights):
    regimes = means.shape[0]
    width = means.shape[1]
    eye = jnp.broadcast_to(jnp.eye(width, dtype=jnp.float32), (regimes, width, width))
    factor = jnp.linalg.cholesky(covs)
    inverse = lax.linalg.triangular_solve(factor, eye, left_side=True, lower=True)
    centred = pcs_t[None, :, :] - means[:, :, None]
    shifted = jnp.einsum("rkj,rjd->rkd", inverse, centred, precision=PRECISE)
    logdet = jnp.sum(jnp.log(jnp.diagonal(factor, axis1=1, axis2=2)), axis=1)
    return jnp.log(weights)[:, None] - logdet[:, None] - 0.5 * jnp.sum(shifted * shifted, axis=1)


def responsibilities(pcs_t, means, covs, weights):
    logp = log_density(pcs_t, means, covs, weights)
    top = jnp.max(logp, axis=0, keepdims=True)
    expo = jnp.exp(logp - top)
    return expo / jnp.sum(expo, axis=0, keepdims=True)


def second_moments(pcs_t, resp, means):
    diff = pcs_t[None, :, :] - means[:, :, None]
    return jnp.einsum("rkd,rjd->rkj", diff * resp[:, None, :], diff, precision=PRECISE)


def total_days(values):
    return lax.psum(values, "day")


def first_moments(pcs_t, resp):
    return lax.dot_general(resp, pcs_t, (((1,), (1,)), ((), ())), precision=PRECISE)


def update(pcs_t, resp, eye):
    counts, sums = total_days((jnp.sum(resp, axis=1), first_moments(pcs_t, resp)))
    counted = jnp.maximum(counts, 1.0)
    means = sums / counted[:, None]
    second = total_days(second_moments(pcs_t, resp, means))
    covs = second / counted[:, None, None] + REG * eye[None]
    weights = counted / jnp.sum(counted)
    return (means, covs, weights)


def body(anomalies, eofs, means_init, variances, mixing):
    width = eofs.shape[0]
    partial_pcs = lax.dot_general(
        anomalies,
        lax.all_gather(eofs, "day", axis=1, tiled=True),
        (((1,), (1,)), ((), ())),
        preferred_element_type=jnp.float32,
    )
    pcs = lax.psum(partial_pcs, "grid")
    pcs_t = pcs.T
    eye = jnp.eye(width, dtype=jnp.float32)
    means = means_init
    covs = variances[:, :, None] * eye[None]
    weights = mixing / jnp.sum(mixing)
    for step in range(ITERS):
        resp = responsibilities(pcs_t, means, covs, weights)
        means, covs, weights = update(pcs_t, resp, eye)
    member = responsibilities(pcs_t, means, covs, weights)
    counts = lax.psum(jnp.sum(member, axis=1), "day")
    counted = jnp.maximum(counts, 1.0)
    terms = jnp.dot(member.astype(jnp.bfloat16), anomalies, preferred_element_type=jnp.float32)
    sums = lax.psum_scatter(terms, "day", scatter_dimension=1, tiled=True)
    composites = (sums / counted[:, None]).astype(jnp.bfloat16)
    return (means, covs, weights, member, composites)


def solution(mesh):
    in_specs = (P("day", "grid"), P(None, ("grid", "day")), P(), P(), P())
    out_specs = (P(), P(), P(), P(None, "day"), P(None, ("grid", "day")))
    return jax.shard_map(body, mesh=mesh, in_specs=in_specs, out_specs=out_specs, check_vma=False)
```

profile of v0, /device:TPU:2, one launch (start us, length us, event | category | flops | bytes accessed | tf_op | source)
XLA Modules:
  0.0 667.7 jit_solution(10305190547740485479)
XLA Ops:
  7.2 21.7 %all_gather.3 = bf16[64,4096]{1,0:T(8,128)(2,1)S(1)} all-gather(bf16[64,256]{1,0:T(8,128)(2,1)} %param.9), channel_id=1, replica_groups=mesh['grid'=16,'day'=16] {'day'}, dimensions={1}, use_global_device_ids=true | all-gather | bytes 557056 | tf_op jit(solution)/shard_map/all_gather | solution.py:57
  28.9 6.8 %fusion.61 = f32[1024,64]{0,1:T(8,128)} fusion(bf16[1024,4096]{1,0:T(8,128)(2,1)} %param.8, bf16[64,4096]{1,0:T(8,128)(2,1)S(1)} %all_gather.3), kind=kOutput, calls=%fused_computation.101 | convolution fusion | flops 536870912 | bytes 9175040 | tf_op jit(solution)/shard_map/dot_general | solution.py:55
  36.0 46.9 %custom-call.16 = f32[8,64,64]{2,1,0:T(8,128)S(1)} custom-call(f32[8,64,64]{2,1,0:T(8,128)S(1)} %fusion.36), custom_call_target="Cholesky" | custom-call | tf_op jit(solution)/shard_map/jit(cholesky)/cholesky | solution.py:15
  86.0 39.3 %custom-call.17 = f32[8,1,64,64]{2,3,1,0:T(8,128)S(1)} custom-call(f32[8,1,64,64]{3,2,1,0:T(8,128)S(1)} %get-tuple-element.33), custom_call_target="InvertDiagBlocksLowerTriangular" | custom-call | tf_op jit(solution)/shard_map/triangular_solve/custom-call.0 | solution.py:16
  125.9 3.6 all-reduce.6.cloned.1.call-done
  129.6 3.0 multiply_reduce_fusion.2
  132.9 1.2 fusion.62
  134.1 25.0 %all-reduce.1 = (f32[8,64]{1,0:T(8,128)S(1)}, f32[8]{0:T(128)S(1)}) all-reduce(f32[8,64]{1,0:T(8,128)S(1)} %fusion.62, f32[8]{0:T(128)S(1)} %get-tuple-element.31), channel_id=1, replica_groups=mesh['grid'=16,'day'=16] {'day'}, use_global_device_ids=true, to_apply=%region_11.0 | all-reduce | flops 520 | bytes 4160 | tf_op jit(solution)/shard_map/psum | solution.py:36
  159.8 4.2 fusion.6
  164.2 107.1 %all-reduce.8.cloned.1.call-done = f32[8,64,64]{1,2,0:T(8,128)} async-done(((f32[8,64,64]{1,2,0:T(8,128)}), f32[8,64,64]{1,2,0:T(8,128)}) %all-reduce.8.cloned.1.call-update) | async-done | bytes 131088 | tf_op jit(solution)/shard_map/psum | solution.py:36
  273.6 46.9 %custom-call.18 = f32[8,64,64]{2,1,0:T(8,128)S(1)} custom-call(f32[8,64,64]{2,1,0:T(8,128)S(1)} %fusion.33), custom_call_target="Cholesky" | custom-call | tf_op jit(solution)/shard_map/jit(cholesky)/cholesky | solution.py:15
  320.8 39.3 %custom-call.19 = f32[8,1,64,64]{2,3,1,0:T(8,128)S(1)} custom-call(f32[8,1,64,64]{3,2,1,0:T(8,128)S(1)} %get-tuple-element.29), custom_call_target="InvertDiagBlocksLowerTriangular" | custom-call | tf_op jit(solution)/shard_map/triangular_solve/custom-call.0 | solution.py:16
  360.8 2.0 multiply_reduce_fusion.1
  365.7 26.9 %all-reduce = (f32[8,64]{1,0:T(8,128)S(1)}, f32[8]{0:T(128)S(1)}) all-reduce(f32[8,64]{1,0:T(8,128)S(1)} %fusion.63, f32[8]{0:T(128)S(1)} %get-tuple-element.27), channel_id=1, replica_groups=mesh['grid'=16,'day'=16] {'day'}, use_global_device_ids=true, to_apply=%region_17.0 | all-reduce | flops 520 | bytes 4160 | tf_op jit(solution)/shard_map/psum | solution.py:36
  393.3 3.1 fusion.2
  396.7 106.8 %all-reduce.10.cloned.1.call-done = f32[8,64,64]{1,2,0:T(8,128)} async-done(((f32[8,64,64]{1,2,0:T(8,128)}), f32[8,64,64]{1,2,0:T(8,128)}) %all-reduce.10.cloned.1.call-update) | async-done | bytes 131088 | tf_op jit(solution)/shard_map/psum | solution.py:36
  504.7 1.2 fusion.30
  505.9 46.9 %custom-call.20 = f32[8,64,64]{2,1,0:T(8,128)S(1)} custom-call(f32[8,64,64]{2,1,0:T(8,128)S(1)} %fusion.30), custom_call_target="Cholesky" | custom-call | tf_op jit(solution)/shard_map/jit(cholesky)/cholesky | solution.py:15
  553.0 39.3 %custom-call.21 = f32[8,1,64,64]{2,3,1,0:T(8,128)S(1)} custom-call(f32[8,1,64,64]{3,2,1,0:T(8,128)S(1)} %get-tuple-element.25), custom_call_target="InvertDiagBlocksLowerTriangular" | custom-call | tf_op jit(solution)/shard_map/triangular_solve/custom-call.0 | solution.py:16
  593.0 2.0 multiply_reduce_fusion
  598.1 5.2 fusion.51
  603.4 26.4 %psum.63 = f32[8]{0:T(128)S(1)} all-reduce(f32[8]{0:T(128)S(1)} %get-tuple-element.21), channel_id=1, replica_groups=mesh['grid'=16,'day'=16] {'day'}, use_global_device_ids=true, to_apply=%region_28.31 | all-reduce | flops 8 | bytes 64 | tf_op jit(solution)/shard_map/psum | solution.py:71
  629.8 30.0 %reduce-scatter.2.cloned.1.call-done = f32[8,256]{1,0:T(8,128)} async-done(((f32[8,4096]{1,0:T(8,128)}), f32[8,256]{1,0:T(8,128)}) %reduce-scatter.2.cloned.1.call-update) | async-done | bytes 8208 | tf_op jit(solution)/shard_map/reduce_scatter | solution.py:74
  659.8 1.4 divide_convert_fusion
  (75 shorter events, 17.4 us)
Async XLA Ops:
  7.2 122.4 %all-reduce.6.cloned.1.call-start = ((), (), s32[]{:S(2)}) async-start(), calls=%async_computation.1 | async-start | bytes 524288 | tf_op jit(solution)/shard_map/psum | solution.py:61
  28.9 6.9 %copy-start.3 = (f32[8,64]{1,0:T(8,128)S(1)}, f32[8,64]{1,0:T(8,128)}, u32[]{:S(2)}) copy-start(f32[8,64]{1,0:T(8,128)} %param.11) | copy-start | bytes 6148
  35.7 235.7 %all-reduce.8.cloned.1.call-start = ((), (), s32[]{:S(2)}) async-start(), calls=%async_computation.2 | async-start | bytes 524288 | tf_op jit(solution)/shard_map/psum | solution.py:36
  35.9 48.8 %copy-start.5 = (f32[8]{0:T(128)S(1)}, f32[8]{0:T(128)}, u32[]{:S(2)}) copy-start(f32[8]{0:T(128)} %param.12) | copy-start | bytes 100
  36.0 93.6 %copy-start.6 = (f32[8,64]{1,0:T(8,128)S(1)}, f32[8,64]{1,0:T(8,128)}, u32[]{:S(2)}) copy-start(f32[8,64]{1,0:T(8,128)} %param.10) | copy-start | bytes 6148
  164.0 196.8 %copy-start = (f32[1024,64]{0,1:T(8,128)S(1)}, f32[1024,64]{0,1:T(8,128)}, u32[]{:S(2)}) copy-start(f32[1024,64]{0,1:T(8,128)} %all-reduce.6.cloned.1.call-done) | copy-start | bytes 786436
  164.0 339.5 %all-reduce.10.cloned.1.call-start = ((), (), s32[]{:S(2)}) async-start(), calls=%async_computation.3 | async-start | bytes 524288 | tf_op jit(solution)/shard_map/psum | solution.py:36
  393.3 199.7 %copy-start.4 = (f32[8,64]{1,0:T(8,128)}, f32[8,64]{1,0:T(8,128)S(1)}, u32[]{:S(2)}) copy-start(f32[8,64]{1,0:T(8,128)S(1)} %broadcast_divide_fusion) | copy-start | bytes 6148
  396.4 263.4 %reduce-scatter.2.cloned.1.call-start = ((), (), s32[]{:S(2)}) async-start(), calls=%async_computation.4 | async-start | bytes 139264 | tf_op jit(solution)/shard_map/reduce_scatter | solution.py:74
  504.7 91.0 %copy-start.1 = (f32[8,64,64]{2,1,0:T(8,128)}, f32[8,64,64]{2,1,0:T(8,128)S(1)}, u32[]{:S(2)}) copy-start(f32[8,64,64]{2,1,0:T(8,128)S(1)} %copy.27) | copy-start | bytes 393220
  598.1 5.3 copy-start.2
Sparse Core Ops, SparseCore 0:
  35.8 93.7 all-reduce.5
  164.1 107.2 all-reduce.7
  396.6 106.8 all-reduce.9
  603.5 56.2 reduce-scatter.1
where the time goes:
time: 668 us
  other arithmetic  271 us (41%)
  waiting for transfers between devices  248 us (37%)
  blocking collectives  100 us (15%)
  matrix products  29.6 us (4%)
  between operations  14.1 us (2%)
    psum x2, waiting for transfers between devices, total_days(): return lax.psum(values, 'day')  214 us
    another operation x10, other arithmetic, log_density(): factor = jnp.linalg.cholesky(covs)  141 us
    another operation x6, other arithmetic, log_density(): lax.linalg.triangular_solve(factor, eye, left_side=True, lower=True)  118 us
    psum x2, blocking collectives, total_days(): return lax.psum(values, 'day')  52 us
    reduce_scatter x1, waiting for transfers between devices, body(): sums = lax.psum_scatter(terms, 'day', scatter_dimension=1, tiled=True)  30 us
    psum x1, blocking collectives, body(): counts = lax.psum(jnp.sum(member, axis=1), 'day')  26.4 us
    all_gather x1, blocking collectives, body(): lax.all_gather(eofs, 'day', axis=1, tiled=True)  21.7 us
  transfers between devices with their start and end apart: 4, of which 4 were waited for; matrix products, arithmetic and copies ran while one was open for 13% of the time, Pallas kernels for 0%

commit v1 on v0

--- a/solution.py
+++ b/solution.py
@@ -6,6 +6,22 @@
 ITERS = 2
 PRECISE = lax.Precision.HIGHEST
 REG = 0.01
+
+
+def ring_gather(x, axis, dim):
+    ways, here, step = (lax.axis_size(axis), lax.axis_index(axis), x.shape[dim])
+    dims = [n * ways if d == dim else n for d, n in enumerate(x.shape)]
+    full = lax.dynamic_update_slice_in_dim(jnp.zeros(dims, x.dtype), x, here * step, axis=dim)
+    going_up = going_down = x
+    for far in range(1, ways // 2 + 1):
+        going_up = lax.ppermute(going_up, axis, [(d, (d + 1) % ways) for d in range(ways)])
+        full = lax.dynamic_update_slice_in_dim(full, going_up, (here - far) % ways * step, axis=dim)
+        if 2 * far < ways:
+            going_down = lax.ppermute(going_down, axis, [(d, (d - 1) % ways) for d in range(ways)])
+            full = lax.dynamic_update_slice_in_dim(
+                full, going_down, (here + far) % ways * step, axis=dim
+            )
+    return full
 
 
 def log_density(pcs_t, means, covs, weights):
@@ -54,7 +70,7 @@
     width = eofs.shape[0]
     partial_pcs = lax.dot_general(
         anomalies,
-        lax.all_gather(eofs, "day", axis=1, tiled=True),
+        ring_gather(eofs, "day", 1),
         (((1,), (1,)), ((), ())),
         preferred_element_type=jnp.float32,
     )

time: 668 us -> 736 us (1.10)
  waiting for transfers between devices: 248 us -> 312 us
  starting transfers between devices: 0.57 us -> 23.6 us
  blocking collectives: 100 us -> 78.3 us
    psum x1, waiting for transfers between devices: 3.6 us -> 51.6 us  [body(): pcs = lax.psum(partial_pcs, 'grid')]
    ppermute x0 -> x15, starting transfers between devices: none -> 23 us  [the longest x7 23 us: ring_gather(): lax.ppermute(going_down, axis, [(d, (d - 1) % ways) for d in range(ways)])]
    all_gather x1 -> x0, blocking collectives: 21.7 us -> none  [body(): lax.all_gather(eofs, 'day', axis=1, tiled=True)]
    ppermute x0 -> x15, waiting for transfers between devices: none -> 16.9 us  [the longest x8 9.05 us: ring_gather(): lax.ppermute(going_up, axis, [(d, (d + 1) % ways) for d in range(ways)])]
  transfers between devices with their start and end apart: 4 -> 19, of which waited for: 4 -> 11; matrix products, arithmetic and copies ran while one was open for 13% -> 12% of each run, Pallas kernels for 0% -> 0%
where the time goes in v1:
time: 736 us
  waiting for transfers between devices  312 us (42%)
  other arithmetic  272 us (37%)
  blocking collectives  78.3 us (11%)
  matrix products  29.6 us (4%)
  starting transfers between devices  23.6 us (3%)
  between operations  14.5 us (2%)
    psum x2, waiting for transfers between devices, total_days(): return lax.psum(values, 'day')  214 us
    another operation x10, other arithmetic, log_density(): factor = jnp.linalg.cholesky(covs)  141 us
    another operation x6, other arithmetic, log_density(): lax.linalg.triangular_solve(factor, eye, left_side=True, lower=True)  118 us
    psum x2, blocking collectives, total_days(): return lax.psum(values, 'day')  51.9 us
    psum x1, waiting for transfers between devices, body(): pcs = lax.psum(partial_pcs, 'grid')  51.6 us
    reduce_scatter x1, waiting for transfers between devices, body(): sums = lax.psum_scatter(terms, 'day', scatter_dimension=1, tiled=True)  30 us
    psum x1, blocking collectives, body(): counts = lax.psum(jnp.sum(member, axis=1), 'day')  26.4 us
    ppermute x7, starting transfers between devices, ring_gather(): lax.ppermute(going_down, axis, [(d, (d - 1) % ways) for d in range(ways)])  23 us
  transfers between devices with their start and end apart: 19, of which 11 were waited for; matrix products, arithmetic and copies ran while one was open for 12% of the time, Pallas kernels for 0%

profile of v1, /device:TPU:2, one launch (start us, length us, event | category | flops | bytes accessed | tf_op | source)
XLA Modules:
  0.0 735.7 jit_solution(17209318686354578293)
XLA Ops:
  7.2 5.3 collective-permute-start.1
  14.2 46.9 %custom-call.16 = f32[8,64,64]{2,1,0:T(8,128)S(1)} custom-call(f32[8,64,64]{2,1,0:T(8,128)S(1)} %fusion.36), custom_call_target="Cholesky" | custom-call | tf_op jit(solution)/shard_map/jit(cholesky)/cholesky | solution.py:31
  68.4 3.0 collective-permute-start.5
  73.0 3.0 collective-permute-start.7
  86.6 3.0 collective-permute-start.13
  89.6 4.5 collective-permute-done.12
  94.2 4.5 collective-permute-done.14
  98.7 6.8 convolution_bitcast_fusion
  106.2 39.3 %custom-call.17 = f32[8,1,64,64]{2,3,1,0:T(8,128)S(1)} custom-call(f32[8,1,64,64]{3,2,1,0:T(8,128)S(1)} %get-tuple-element.33), custom_call_target="InvertDiagBlocksLowerTriangular" | custom-call | tf_op jit(solution)/shard_map/triangular_solve/custom-call.0 | solution.py:32
  146.1 51.6 %all-reduce.6.cloned.1.call-done = f32[1024,64]{0,1:T(8,128)} async-done(((f32[1024,64]{0,1:T(8,128)}), f32[1024,64]{0,1:T(8,128)}) %all-reduce.6.cloned.1.call-update) | async-done | bytes 262160 | tf_op jit(solution)/shard_map/psum | solution.py:77
  197.8 3.0 multiply_reduce_fusion.2
  202.3 25.0 %all-reduce.1 = (f32[8,64]{1,0:T(8,128)S(1)}, f32[8]{0:T(128)S(1)}) all-reduce(f32[8,64]{1,0:T(8,128)S(1)} %fusion.61, f32[8]{0:T(128)S(1)} %get-tuple-element.31), channel_id=1, replica_groups=mesh['grid'=16,'day'=16] {'day'}, use_global_device_ids=true, to_apply=%region_11.14 | all-reduce | flops 520 | bytes 4160 | tf_op jit(solution)/shard_map/psum | solution.py:52
  228.0 4.2 fusion.6
  232.4 107.1 %all-reduce.8.cloned.1.call-done = f32[8,64,64]{1,2,0:T(8,128)} async-done(((f32[8,64,64]{1,2,0:T(8,128)}), f32[8,64,64]{1,2,0:T(8,128)}) %all-reduce.8.cloned.1.call-update) | async-done | bytes 131088 | tf_op jit(solution)/shard_map/psum | solution.py:52
  341.8 46.9 %custom-call.18 = f32[8,64,64]{2,1,0:T(8,128)S(1)} custom-call(f32[8,64,64]{2,1,0:T(8,128)S(1)} %fusion.33), custom_call_target="Cholesky" | custom-call | tf_op jit(solution)/shard_map/jit(cholesky)/cholesky | solution.py:31
  389.0 39.3 %custom-call.19 = f32[8,1,64,64]{2,3,1,0:T(8,128)S(1)} custom-call(f32[8,1,64,64]{3,2,1,0:T(8,128)S(1)} %get-tuple-element.29), custom_call_target="InvertDiagBlocksLowerTriangular" | custom-call | tf_op jit(solution)/shard_map/triangular_solve/custom-call.0 | solution.py:32
  433.8 26.9 %all-reduce = (f32[8,64]{1,0:T(8,128)S(1)}, f32[8]{0:T(128)S(1)}) all-reduce(f32[8,64]{1,0:T(8,128)S(1)} %fusion.62, f32[8]{0:T(128)S(1)} %get-tuple-element.27), channel_id=1, replica_groups=mesh['grid'=16,'day'=16] {'day'}, use_global_device_ids=true, to_apply=%region_17.20 | all-reduce | flops 520 | bytes 4160 | tf_op jit(solution)/shard_map/psum | solution.py:52
  461.5 3.1 fusion.2
  464.9 106.6 %all-reduce.10.cloned.1.call-done = f32[8,64,64]{1,2,0:T(8,128)} async-done(((f32[8,64,64]{1,2,0:T(8,128)}), f32[8,64,64]{1,2,0:T(8,128)}) %all-reduce.10.cloned.1.call-update) | async-done | bytes 131088 | tf_op jit(solution)/shard_map/psum | solution.py:52
  573.9 46.9 %custom-call.20 = f32[8,64,64]{2,1,0:T(8,128)S(1)} custom-call(f32[8,64,64]{2,1,0:T(8,128)S(1)} %fusion.30), custom_call_target="Cholesky" | custom-call | tf_op jit(solution)/shard_map/jit(cholesky)/cholesky | solution.py:31
  621.1 39.3 %custom-call.21 = f32[8,1,64,64]{2,3,1,0:T(8,128)S(1)} custom-call(f32[8,1,64,64]{3,2,1,0:T(8,128)S(1)} %get-tuple-element.25), custom_call_target="InvertDiagBlocksLowerTriangular" | custom-call | tf_op jit(solution)/shard_map/triangular_solve/custom-call.0 | solution.py:32
  666.2 5.2 fusion.51
  671.4 26.4 %psum.63 = f32[8]{0:T(128)S(1)} all-reduce(f32[8]{0:T(128)S(1)} %get-tuple-element.21), channel_id=1, replica_groups=mesh['grid'=16,'day'=16] {'day'}, use_global_device_ids=true, to_apply=%region_28.31 | all-reduce | flops 8 | bytes 64 | tf_op jit(solution)/shard_map/psum | solution.py:87
  697.8 30.0 %reduce-scatter.2.cloned.1.call-done = f32[8,256]{1,0:T(8,128)} async-done(((f32[8,4096]{1,0:T(8,128)}), f32[8,256]{1,0:T(8,128)}) %reduce-scatter.2.cloned.1.call-update) | async-done | bytes 8208 | tf_op jit(solution)/shard_map/reduce_scatter | solution.py:90
  (121 shorter events, 43.4 us)
Async XLA Ops:
  7.2 190.6 %all-reduce.6.cloned.1.call-start = ((), (), s32[]{:S(2)}) async-start(), calls=%async_computation.1 | async-start | bytes 524288 | tf_op jit(solution)/shard_map/psum | solution.py:77
  7.2 56.7 %collective-permute-start.1 = (bf16[64,256]{1,0:T(8,128)(2,1)}, bf16[64,256]{1,0:T(8,128)(2,1)S(1)}, u32[]{:S(2)}, u32[]{:S(2)}) collective-permute-start(bf16[64,256]{1,0:T(8,128)(2,1)} %param.9), channel_id=1, source_target_pairs={{0,15},{1,0},{2,1},{3,2},{4,3},{5,4},{6,5},{7,6},{8,7},{9,8},{10,9... | collective-permute-start | bytes 98312 | tf_op jit(solution)/shard_map/ppermute | solution.py:20
  12.5 54.3 %collective-permute-start = (bf16[64,256]{1,0:T(8,128)(2,1)}, bf16[64,256]{1,0:T(8,128)(2,1)S(1)}, u32[]{:S(2)}, u32[]{:S(2)}) collective-permute-start(bf16[64,256]{1,0:T(8,128)(2,1)} %param.9), channel_id=1, source_target_pairs={{0,1},{1,2},{2,3},{3,4},{4,5},{5,6},{6,7},{7,8},{8,9},{9,10},{10,1... | collective-permute-start | bytes 98312 | tf_op jit(solution)/shard_map/ppermute | solution.py:17
  14.2 48.8 %copy-start.3 = (bf16[64,256]{1,0:T(8,128)(2,1)S(1)}, bf16[64,256]{1,0:T(8,128)(2,1)}, u32[]{:S(2)}) copy-start(bf16[64,256]{1,0:T(8,128)(2,1)} %param.9) | copy-start | bytes 98308
  63.9 4.5 collective-permute-start.3
  66.8 4.6 collective-permute-start.2
  68.4 4.6 collective-permute-start.5
  71.4 4.6 collective-permute-start.4
  73.0 4.6 collective-permute-start.7
  75.9 4.6 collective-permute-start.6
  77.5 4.6 collective-permute-start.9
  80.5 4.6 collective-permute-start.8
  82.1 4.6 collective-permute-start.11
  85.0 4.6 collective-permute-start.10
  86.6 7.5 %collective-permute-start.13 = (bf16[64,256]{1,0:T(8,128)(2,1)S(1)}, bf16[64,256]{1,0:T(8,128)(2,1)S(1)}, u32[]{:S(2)}, u32[]{:S(2)}) collective-permute-start(bf16[64,256]{1,0:T(8,128)(2,1)S(1)} %collective-permute-done.11), channel_id=1, source_target_pairs={{0,15},{1,0},{2,1},{3,2},{4,3},{5,4},{6,5},{7,6},{8,7},{9,8},{10,9... | collective-permute-start | bytes 98312 | tf_op jit(solution)/shard_map/ppermute | solution.py:20
  89.6 4.6 collective-permute-start.12
  94.1 4.6 collective-permute-start.14
  98.7 99.1 %copy-start.6 = (f32[8,64]{1,0:T(8,128)S(1)}, f32[8,64]{1,0:T(8,128)}, u32[]{:S(2)}) copy-start(f32[8,64]{1,0:T(8,128)} %param.10) | copy-start | bytes 6148
  105.5 234.1 %all-reduce.8.cloned.1.call-start = ((), (), s32[]{:S(2)}) async-start(), calls=%async_computation.2 | async-start | bytes 524288 | tf_op jit(solution)/shard_map/psum | solution.py:52
  232.2 196.8 %copy-start = (f32[1024,64]{0,1:T(8,128)S(1)}, f32[1024,64]{0,1:T(8,128)}, u32[]{:S(2)}) copy-start(f32[1024,64]{0,1:T(8,128)} %all-reduce.6.cloned.1.call-done) | copy-start | bytes 786436
  232.2 339.3 %all-reduce.10.cloned.1.call-start = ((), (), s32[]{:S(2)}) async-start(), calls=%async_computation.3 | async-start | bytes 524288 | tf_op jit(solution)/shard_map/psum | solution.py:52
  461.5 199.6 %copy-start.4 = (f32[8,64]{1,0:T(8,128)}, f32[8,64]{1,0:T(8,128)S(1)}, u32[]{:S(2)}) copy-start(f32[8,64]{1,0:T(8,128)S(1)} %broadcast_divide_fusion) | copy-start | bytes 6148
  464.6 263.2 %reduce-scatter.2.cloned.1.call-start = ((), (), s32[]{:S(2)}) async-start(), calls=%async_computation.4 | async-start | bytes 139264 | tf_op jit(solution)/shard_map/reduce_scatter | solution.py:90
  572.7 91.0 %copy-start.1 = (f32[8,64,64]{2,1,0:T(8,128)}, f32[8,64,64]{2,1,0:T(8,128)S(1)}, u32[]{:S(2)}) copy-start(f32[8,64,64]{2,1,0:T(8,128)S(1)} %copy.27) | copy-start | bytes 393220
  (2 other events, 7.3 us)
Sparse Core Ops, SparseCore 0:
  105.6 92.1 all-reduce.5
  232.3 107.1 all-reduce.7
  464.7 106.7 all-reduce.9
  671.5 56.2 reduce-scatter.1
